TPU v7x, 256 devices: a whole 4x4x8 slice. The times are simulated.
256 devices in a mesh: tok: 32 (over y, z), voc: 8 (over x, core).
Axes of the slice: x: 4, y: 4, z: 8, core: 2. Of those that a mesh axis runs over, the one named last changes fastest.
Arguments:
- teacher_rows: bfloat16 [8192, 2048], P('tok', 'voc')
- drafter_rows: bfloat16 [8192, 2048], P('tok', 'voc')
- head: bfloat16 [2048, 16384], P(None, 'voc'), may hold values from -1 to 1
- fr_ids: int32 [16384], P('voc'), may hold values from 0 to 151935, as said below
- targets: int32 [8192], P('tok'), may hold values from 0 to 151935
- dest_index: int32 [8192], P('tok'), may hold values from -1 to 8191, as said below
- counts: int32 [32], replicated, may hold values from 64 to 256, as said below
Outputs:
- row_loss: float32 [8192], P('tok')
- drafter_grad: bfloat16 [8192, 2048], P('tok', 'voc')
Inputs may be any that keep to these rules, and one draw needn't show every extreme that they name: `dest_index`: the prefill rows that name a slot name distinct slots. With blocks of 256 rows and 32 blocks, a row of prefill block b names a slot of drafter block (b + k) mod 32 for k in 0, 1, 16, 17; at most 64 rows go from one prefill block to one drafter block, and every drafter block receives exactly 64 from its own prefill block. The slots named in drafter block j are exactly its first counts[j] slots, grouped by k in that order. counts[j] is the number of prefill rows that name a slot of block j; some block is full. `fr_ids`: distinct ids.
All inputs are finite; a program needn't handle non-finite values.
Results may differ from a plain program's by a relative error of at most 0.0041.
Values may be sent and summed in bfloat16 or wider, within the bound.
A program may use at most 64 MiB of HBM per device.

v0:
```python
import jax
import jax.numpy as jnp
from jax import lax
from jax.sharding import PartitionSpec as P

loss_scale = 16.0


def encode(values):
    return jnp.stack([values // 128, values % 128], axis=1).astype(jnp.float32).astype(jnp.bfloat16)


def decode(code):
    widened = code.astype(jnp.float32)
    return (widened[:, 0] * 128.0 + widened[:, 1]).astype(jnp.int32)


def per_device(teacher_rows, drafter_rows, head, fr_ids, targets, dest_index, counts):
    row_count = teacher_rows.shape[0]
    tok_index = lax.axis_index("tok")
    first_slot = tok_index * row_count
    slot_ids = jnp.arange(row_count, dtype=jnp.int32)
    code = encode(dest_index + 1)
    rows_piece = lax.all_gather(teacher_rows, "tok", axis=0, tiled=True)
    code_piece = lax.all_gather(code, "tok", axis=0, tiled=True)
    wanted = decode(code_piece) - 1 - first_slot
    select = (slot_ids[:, None] == wanted[None, :]).astype(jnp.bfloat16)
    moved = jnp.dot(select, rows_piece, preferred_element_type=jnp.float32).astype(jnp.bfloat16)
    teacher_full, drafter_full = (
        lax.all_gather(moved, "voc", axis=1, tiled=True),
        lax.all_gather(drafter_rows, "voc", axis=1, tiled=True),
    )
    teach_logit = jnp.dot(teacher_full, head, preferred_element_type=jnp.float32)
    draft_logit = jnp.dot(drafter_full, head, preferred_element_type=jnp.float32)
    hit_table = (targets[:, None] == fr_ids[None, :]).astype(jnp.float32)
    local_hits = jnp.sum(hit_table, axis=1)
    local_target = jnp.sum(hit_table * draft_logit, axis=1)
    teach_max, draft_max = lax.pmax(
        (jnp.max(teach_logit, axis=1), jnp.max(draft_logit, axis=1)), "voc"
    )
    teach_exp = jnp.exp(teach_logit - teach_max[:, None])
    draft_exp = jnp.exp(draft_logit - draft_max[:, None])
    teach_total, draft_total, cross, target_logit, hits = lax.psum(
        (
            jnp.sum(teach_exp, axis=1),
            jnp.sum(draft_exp, axis=1),
            jnp.sum(teach_exp * (teach_logit - draft_logit), axis=1),
            local_target,
            local_hits,
        ),
        "voc",
    )
    valid = (slot_ids < counts[tok_index]).astype(jnp.float32)
    teach_lse = teach_max + jnp.log(teach_total)
    draft_lse = draft_max + jnp.log(draft_total)
    row_loss = valid * (
        cross / teach_total - teach_lse + draft_lse + hits * (draft_lse - target_logit)
    )
    teach_prob = teach_exp / teach_total[:, None]
    draft_prob = draft_exp / draft_total[:, None]
    grad_logit = (
        valid[:, None] * ((1.0 + hits)[:, None] * draft_prob - teach_prob - hit_table)
    ).astype(jnp.bfloat16)
    summed = lax.psum_scatter(
        lax.dot_general(
            head, grad_logit, (((1,), (1,)), ((), ())), preferred_element_type=jnp.float32
        ),
        "voc",
        scatter_dimension=0,
        tiled=True,
    )
    drafter_grad = (loss_scale * summed).T.astype(jnp.bfloat16)
    return (row_loss, drafter_grad)


def solution(mesh):
    return jax.shard_map(
        per_device,
        mesh=mesh,
        in_specs=(
            P("tok", "voc"),
            P("tok", "voc"),
            P(None, "voc"),
            P("voc"),
            P("tok"),
            P("tok"),
            P(),
        ),
        out_specs=(P("tok"), P("tok", "voc")),
        check_vma=False,
    )
```

profile of v0, /device:TPU:8, one launch (start us, length us, event | category | flops | bytes accessed | tf_op | source)
XLA Modules:
  0.0 239.7 jit_solution(6944104512413968319)
XLA Ops:
  7.2 0.0 all-gather.4.cloned.1.call-start
  7.2 0.7 all-gather.4.cloned.1.call-update
  7.9 0.0 all-gather.8.cloned.1.call-start
  7.9 0.7 all-gather.8.cloned.1.call-update
  8.6 0.0 all-gather.6.cloned.1.call-start
  8.7 0.7 and_select_fusion.1
  9.4 45.7 %all_gather.12 = bf16[8192,2]{0,1:T(2,128)(2,1)S(1)} all-gather(bf16[256,2]{0,1:T(2,128)(2,1)S(1)} %fusion.21), channel_id=1, replica_groups=mesh['tok'=32,'voc'=8] {'tok'}, dimensions={0}, use_global_device_ids=true | all-gather | bytes 33792 | tf_op jit(solution)/shard_map/all_gather | solution.py:25
  55.1 0.1 fusion.20
  55.2 38.8 %all-gather.4.cloned.1.call-done = bf16[8192,256]{1,0:T(8,128)(2,1)} async-done(((bf16[256,256]{1,0:T(8,128)(2,1)}), bf16[8192,256]{1,0:T(8,128)(2,1)}) %all-gather.4.cloned.1.call-update) | async-done | bytes 4194320 | tf_op jit(solution)/shard_map/all_gather | solution.py:24
  94.0 0.0 copy-start.2
  94.0 4.1 %fusion.7 = bf16[256,256]{1,0:T(8,128)(2,1)} fusion(bf16[8192,256]{1,0:T(8,128)(2,1)} %all-gather.4.cloned.1.call-done, s32[8192]{0:T(1024)S(1)} %bitcast.14), kind=kOutput, calls=%fused_computation.15 | convolution fusion | flops 1075904512 | bytes 4358144 | tf_op jit(solution)/shard_map/dot_general | solution.py:28
  98.2 0.0 all-gather.6.cloned.1.call-update
  98.2 0.0 reduce-scatter.2.cloned.1.call-start
  98.2 0.0 copy-done.2
  98.2 0.6 dynamic_slice.3
  98.8 0.5 fusion.22
  99.4 21.0 %all-gather.8.cloned.1.call-done = bf16[256,2048]{1,0:T(8,128)(2,1)} async-done(((bf16[256,256]{1,0:T(8,128)(2,1)}), bf16[256,2048]{1,0:T(8,128)(2,1)}) %all-gather.8.cloned.1.call-update) | async-done | bytes 1048592 | tf_op jit(solution)/shard_map/all_gather | solution.py:31
  120.3 6.1 %fusion.24 = (f32[256]{0:T(256)S(1)}, f32[256,2048]{1,0:T(8,128)S(1)}) fusion(bf16[256,2048]{1,0:T(8,128)(2,1)} %all-gather.8.cloned.1.call-done, bf16[2048,2048]{1,0:T(8,128)(2,1)} %param.9), kind=kOutput, calls=%fused_computation.45 | convolution fusion | flops 2148007680 | bytes 11535360 | tf_op jit(solution)/shard_map/dot_general | solution.py:34
  126.4 0.0 copy-start
  126.5 0.0 copy-start.1
  126.5 23.2 %all-gather.6.cloned.1.call-done = bf16[256,2048]{1,0:T(8,128)(2,1)} async-done(((bf16[256,256]{1,0:T(8,128)(2,1)}), bf16[256,2048]{1,0:T(8,128)(2,1)}) %all-gather.6.cloned.1.call-update) | async-done | bytes 1048592 | tf_op jit(solution)/shard_map/all_gather | solution.py:30
  149.7 7.4 %fusion.23 = (f32[256]{0:T(256)S(1)}, f32[256,2048]{1,0:T(8,128)}) fusion(bf16[256,2048]{1,0:T(8,128)(2,1)} %all-gather.6.cloned.1.call-done, bf16[2048,2048]{1,0:T(8,128)(2,1)} %param.9), kind=kOutput, calls=%fused_computation.44 | convolution fusion | flops 2148007680 | bytes 11535360 | tf_op jit(solution)/shard_map/dot_general | solution.py:33
  157.1 14.3 %all-reduce.1 = (f32[256]{0:T(256)S(1)}, f32[256]{0:T(256)S(1)}) all-reduce(f32[256]{0:T(256)S(1)} %get-tuple-element.18, f32[256]{0:T(256)S(1)} %get-tuple-element.20), channel_id=1, replica_groups=mesh['tok'=32,'voc'=8] {'voc'}, use_global_device_ids=true, to_apply=%region_1.2 | all-reduce | flops 512 | bytes 4096 | tf_op jit(solution)/shard_map/pmax | solution.py:38
  171.4 0.0 copy-done
  171.4 0.0 copy-done.1
  171.4 3.0 %multiply_reduce_fusion = (f32[256]{0:T(256)S(1)}, f32[256]{0:T(256)S(1)}, f32[256]{0:T(256)S(1)}, f32[256]{0:T(256)S(1)}, f32[256]{0:T(256)S(1)}) fusion(f32[256,2048]{1,0:T(8,128)} %get-tuple-element.19, f32[256,2048]{1,0:T(8,128)S(1)} %get-tuple-element.21, f32[256]{0:T(256)S(1)} %get-tuple-element.12, s32[2048]{0:T(1024)S(1)} %copy-done, ...), kind=kLoop, calls=%fused_computation.11 | loop fusion | flops 6290176 | bytes 4210688 | tf_op jit(solution)/shard_map/reduce_sum | solution.py:47
  174.4 12.6 %all-reduce = (f32[256]{0:T(256)S(1)}, f32[256]{0:T(256)S(1)}, f32[256]{0:T(256)S(1)}, f32[256]{0:T(256)S(1)}, f32[256]{0:T(256)S(1)}) all-reduce(f32[256]{0:T(256)S(1)} %get-tuple-element.6, f32[256]{0:T(256)S(1)} %get-tuple-element.4, f32[256]{0:T(256)S(1)} %get-tuple-element.5, ...), channel_id=1, replica_groups=mesh['tok'=32,'voc'=8] {'voc'}, use_global_device_ids=true, to_apply=%region_11.12 | all-reduce | flops 1280 | bytes 10240 | tf_op jit(solution)/shard_map/psum | solution.py:43
  187.1 1.1 broadcast_add_fusion
  188.2 8.3 %convolution_bitcast_fusion = f32[2048,256]{0,1:T(8,128)} fusion(bf16[2048,2048]{1,0:T(8,128)(2,1)} %param.9, f32[256,2048]{1,0:T(8,128)} %get-tuple-element.19, f32[256,2048]{1,0:T(8,128)S(1)} %get-tuple-element.21, f32[256]{0:T(256)S(1)} %get-tuple-element.10, f32[256]{0:T(256)S(1)} %get-tuple-element.9, f32[256]{0:T(256)S(1)} %get-tuple-element.14, ...), kind=kOutput, calls=%fused_computation.6 | convolution fusion | flops 2153250816 | bytes 14695424 | tf_op jit(solution)/shard_map/dot_general | solution.py:65
  196.4 0.0 reduce-scatter.2.cloned.1.call-update
  196.5 35.1 %reduce-scatter.2.cloned.1.call-done = f32[256,256]{0,1:T(8,128)} async-done(((f32[2048,256]{0,1:T(8,128)}), f32[256,256]{0,1:T(8,128)}) %reduce-scatter.2.cloned.1.call-update) | async-done | bytes 262160 | tf_op jit(solution)/shard_map/reduce_scatter | solution.py:64
  231.6 1.6 fusion.17
  (2 shorter events, 0.0 us)
Async XLA Ops:
  7.2 86.9 %all-gather.4.cloned.1.call-start = ((), (), s32[]{:S(2)}) async-start(), calls=%async_computation.1 | async-start | bytes 4325376 | tf_op jit(solution)/shard_map/all_gather | solution.py:24
  7.9 112.4 %all-gather.8.cloned.1.call-start = ((), (), s32[]{:S(2)}) async-start(), calls=%async_computation.3 | async-start | bytes 1179648 | tf_op jit(solution)/shard_map/all_gather | solution.py:31
  8.6 141.0 %all-gather.6.cloned.1.call-start = ((), (), s32[]{:S(2)}) async-start(), calls=%async_computation.2 | async-start | bytes 1179648 | tf_op jit(solution)/shard_map/all_gather | solution.py:30
  94.0 4.2 %copy-start.2 = (s32[32]{0:T(128)S(1)}, s32[32]{0:T(128)}, u32[]{:S(2)}) copy-start(s32[32]{0:T(128)} %param.13) | copy-start | bytes 388
  98.2 133.4 %reduce-scatter.2.cloned.1.call-start = ((), (), s32[]{:S(2)}) async-start(), calls=%async_computation.4 | async-start | bytes 2359296 | tf_op jit(solution)/shard_map/reduce_scatter | solution.py:64
  126.4 44.9 %copy-start = (s32[2048]{0:T(1024)S(1)}, s32[2048]{0:T(1024)}, u32[]{:S(2)}) copy-start(s32[2048]{0:T(1024)} %param.10) | copy-start | bytes 24580
  126.5 44.9 %copy-start.1 = (s32[256]{0:T(256)S(1)}, s32[256]{0:T(256)}, u32[]{:S(2)}) copy-start(s32[256]{0:T(256)} %param.11) | copy-start | bytes 3076
Sparse Core Ops, SparseCore 0:
  10.6 83.4 all-gather.3
  95.9 24.3 all-gather.7
  122.7 26.8 all-gather.5
  196.6 34.9 reduce-scatter.1
where the time goes:
time: 240 us
  waiting for transfers between devices  120 us (50%)
  blocking collectives  72.6 us (30%)
  matrix products  25.9 us (11%)
  between operations  13.8 us (6%)
  other arithmetic  7.13 us (3%)
    all_gather x1, blocking collectives, per_device(): code_piece = lax.all_gather(code, 'tok', axis=0, tiled=True)  45.7 us
    all_gather x1, waiting for transfers between devices, per_device(): rows_piece = lax.all_gather(teacher_rows, 'tok', axis=0, tiled=True)  38.8 us
    reduce_scatter x1, waiting for transfers between devices, per_device(): lax.psum_scatter(lax.dot_general(head, grad_logit, (((1,), (1,)), ((), ()...  35.1 us
    all_gather x1, waiting for transfers between devices, per_device(): lax.all_gather(moved, 'voc', axis=1, tiled=True)  23.2 us
    all_gather x1, waiting for transfers between devices, per_device(): lax.all_gather(drafter_rows, 'voc', axis=1, tiled=True)  21 us
    pmax x1, blocking collectives, per_device(): lax.pmax((jnp.max(teach_logit, axis=1), jnp.max(draft_logit, axis=1)), 'v...  14.3 us
    psum x1, blocking collectives, per_device(): lax.psum((jnp.sum(teach_exp, axis=1), jnp.sum(draft_exp, axis=1), jnp.sum...  12.6 us
    dot_general x1, matrix products, per_device(): lax.dot_general(head, grad_logit, (((1,), (1,)), ((), ())), preferred_ele...  8.27 us
  transfers between devices with their start and end apart: 4, of which 4 were waited for; matrix products, arithmetic and copies ran while one was open for 5% of the time, Pallas kernels for 0%

commit v1 on v0

--- a/solution.py
+++ b/solution.py
@@ -4,6 +4,19 @@
 from jax.sharding import PartitionSpec as P
 
 loss_scale = 16.0
+
+
+def ring_gather(x, axis, dim):
+    ways = lax.axis_size(axis)
+    up = [(d, (d + 1) % ways) for d in range(ways)]
+    down = [(d, (d - 1) % ways) for d in range(ways)]
+    earlier, later = ([x], [x])
+    for _ in range(ways // 2):
+        earlier.append(lax.ppermute(earlier[-1], axis, up))
+    for _ in range((ways - 1) // 2):
+        later.append(lax.ppermute(later[-1], axis, down))
+    line = jnp.concatenate([*earlier[::-1], *later[1:]], axis=dim)
+    return jnp.roll(line, (lax.axis_index(axis) - ways // 2) * x.shape[dim], axis=dim)
 
 
 def encode(values):
@@ -28,7 +41,7 @@
     moved = jnp.dot(select, rows_piece, preferred_element_type=jnp.float32).astype(jnp.bfloat16)
     teacher_full, drafter_full = (
         lax.all_gather(moved, "voc", axis=1, tiled=True),
-        lax.all_gather(drafter_rows, "voc", axis=1, tiled=True),
+        ring_gather(drafter_rows, "voc", 1),
     )
     teach_logit = jnp.dot(teacher_full, head, preferred_element_type=jnp.float32)
     draft_logit = jnp.dot(drafter_full, head, preferred_element_type=jnp.float32)

time: 240 us -> 213 us (0.89)
  waiting for transfers between devices: 120 us -> 73.1 us
  local copies, waits for them, and re-layouts: 0.57 us -> 13.1 us
  starting transfers between devices: 0.16 us -> 7.08 us
    all_gather x1, waiting for transfers between devices: 38.8 us -> 17.2 us  [per_device(): rows_piece = lax.all_gather(teacher_rows, 'tok', axis=0, tiled=True)]
    all_gather x1 -> x0, waiting for transfers between devices: 21 us -> none  [per_device(): lax.all_gather(drafter_rows, 'voc', axis=1, tiled=True)]
    all_gather x1, waiting for transfers between devices: 23.2 us -> 11.5 us  [per_device(): lax.all_gather(moved, 'voc', axis=1, tiled=True)]
    unnamed x6 -> x21, local copies, waits for them, and re-layouts: 0.02 us -> 11.2 us
    ppermute x0 -> x7, waiting for transfers between devices: none -> 8.54 us  [the longest x4 8.45 us: ring_gather(): earlier.append(lax.ppermute(earlier[-1], axis, up))]
    ppermute x0 -> x7, starting transfers between devices: none -> 6.96 us  [the longest x3 6.45 us: ring_gather(): later.append(lax.ppermute(later[-1], axis, down))]
  transfers between devices with their start and end apart: 4 -> 10, of which waited for: 4 -> 6; matrix products, arithmetic and copies ran while one was open for 5% -> 12% of each run, Pallas kernels for 0% -> 0%
where the time goes in v1:
time: 213 us
  waiting for transfers between devices  73.1 us (34%)
  blocking collectives  72.6 us (34%)
  matrix products  26 us (12%)
  between operations  13.9 us (7%)
  local copies, waits for them, and re-layouts  13.1 us (6%)
  other arithmetic  7.19 us (3%)
  starting transfers between devices  7.08 us (3%)
    all_gather x1, blocking collectives, per_device(): code_piece = lax.all_gather(code, 'tok', axis=0, tiled=True)  45.7 us
    reduce_scatter x1, waiting for transfers between devices, per_device(): lax.psum_scatter(lax.dot_general(head, grad_logit, (((1,), (1,)), ((), ()...  35.1 us
    all_gather x1, waiting for transfers between devices, per_device(): rows_piece = lax.all_gather(teacher_rows, 'tok', axis=0, tiled=True)  17.2 us
    pmax x1, blocking collectives, per_device(): lax.pmax((jnp.max(teach_logit, axis=1), jnp.max(draft_logit, axis=1)), 'v...  14.3 us
    psum x1, blocking collectives, per_device(): lax.psum((jnp.sum(teach_exp, axis=1), jnp.sum(draft_exp, axis=1), jnp.sum...  12.6 us
    all_gather x1, waiting for transfers between devices, per_device(): lax.all_gather(moved, 'voc', axis=1, tiled=True)  11.5 us
    unnamed x21, local copies, waits for them, and re-layouts  11.2 us
    ppermute x4, waiting for transfers between devices, ring_gather(): earlier.append(lax.ppermute(earlier[-1], axis, up))  8.45 us
  transfers between devices with their start and end apart: 10, of which 6 were waited for; matrix products, arithmetic and copies ran while one was open for 12% of the time, Pallas kernels for 0%

profile of v1, /device:TPU:8, one launch (start us, length us, event | category | flops | bytes accessed | tf_op | source)
XLA Modules:
  0.0 212.9 jit_solution(12431958404959278540)
XLA Ops:
  7.2 0.0 all-gather.3.cloned.1.call-start
  7.2 0.7 all-gather.3.cloned.1.call-update
  7.9 0.0 all-gather.5.cloned.1.call-start
  7.9 0.0 collective-permute-start
  8.0 5.8 %collective-permute-done = bf16[256,256]{1,0:T(8,128)(2,1)S(1)} collective-permute-done((bf16[256,256]{1,0:T(8,128)(2,1)}, bf16[256,256]{1,0:T(8,128)(2,1)S(1)}, u32[]{:S(2)}, u32[]{:S(2)}) %collective-permute-start) | collective-permute-done | bytes 131104 | tf_op jit(solution)/shard_map/ppermute | solution.py:15
  13.8 0.0 collective-permute-start.1
  13.8 3.0 %collective-permute-start.4 = (bf16[256,256]{1,0:T(8,128)(2,1)}, bf16[256,256]{1,0:T(8,128)(2,1)S(1)}, u32[]{:S(2)}, u32[]{:S(2)}) collective-permute-start(bf16[256,256]{1,0:T(8,128)(2,1)} %param.8), channel_id=1, source_target_pairs={{0,7},{1,0},{2,1},{3,2},{4,3},{5,4},{6,5},{7,6},{8,15},{9,8},{10,9... | collective-permute-start | bytes 393224 | tf_op jit(solution)/shard_map/ppermute | solution.py:17
  16.7 2.6 %collective-permute-done.1 = bf16[256,256]{1,0:T(8,128)(2,1)S(1)} collective-permute-done((bf16[256,256]{1,0:T(8,128)(2,1)S(1)}, bf16[256,256]{1,0:T(8,128)(2,1)S(1)}, u32[]{:S(2)}, u32[]{:S(2)}) %collective-permute-start.1) | collective-permute-done | bytes 131104 | tf_op jit(solution)/shard_map/ppermute | solution.py:15
  19.4 0.0 collective-permute-start.2
  19.4 0.7 and_select_fusion.1
  20.1 45.7 %all_gather.9 = bf16[8192,2]{0,1:T(2,128)(2,1)S(1)} all-gather(bf16[256,2]{0,1:T(2,128)(2,1)S(1)} %fusion.23), channel_id=1, replica_groups=mesh['tok'=32,'voc'=8] {'tok'}, dimensions={0}, use_global_device_ids=true | all-gather | bytes 33792 | tf_op jit(solution)/shard_map/all_gather | solution.py:38
  65.8 0.0 collective-permute-done.4
  65.8 0.0 collective-permute-start.5
  65.8 0.0 collective-permute-done.2
  65.8 0.5 collective-permute-start.3
  66.3 0.1 fusion.22
  66.4 1.2 dynamic_slice.7
  67.7 0.6 fusion.24
  68.3 0.1 collective-permute-done.5
  68.3 3.5 %collective-permute-start.6 = (bf16[256,256]{1,0:T(8,128)(2,1)S(1)}, bf16[256,256]{1,0:T(8,128)(2,1)S(1)}, u32[]{:S(2)}, u32[]{:S(2)}) collective-permute-start(bf16[256,256]{1,0:T(8,128)(2,1)S(1)} %collective-permute-done.5), channel_id=1, source_target_pairs={{0,7},{1,0},{2,1},{3,2},{4,3},{5,4},{6,5},{7,6},{8,15},{9,8},{10,9... | collective-permute-start | bytes 393224 | tf_op jit(solution)/shard_map/ppermute | solution.py:17
  71.8 0.0 collective-permute-done.3
  71.8 0.7 constant_dynamic-update-slice_fusion.15
  72.5 0.7 constant_dynamic-update-slice_fusion.14
  73.2 0.7 constant_dynamic-update-slice_fusion.13
  73.9 0.7 constant_dynamic-update-slice_fusion.12
  74.6 1.6 constant_dynamic-update-slice_fusion.11
  76.2 0.7 constant_dynamic-update-slice_fusion.10
  76.9 17.2 %all-gather.3.cloned.1.call-done = bf16[8192,256]{1,0:T(8,128)(2,1)} async-done(((bf16[256,256]{1,0:T(8,128)(2,1)}), bf16[8192,256]{1,0:T(8,128)(2,1)}) %all-gather.3.cloned.1.call-update) | async-done | bytes 4194320 | tf_op jit(solution)/shard_map/all_gather | solution.py:37
  94.1 0.0 copy-start
  94.1 4.1 %fusion.7 = bf16[256,256]{1,0:T(8,128)(2,1)} fusion(bf16[8192,256]{1,0:T(8,128)(2,1)} %all-gather.3.cloned.1.call-done, s32[8192]{0:T(1024)S(1)} %bitcast.13), kind=kOutput, calls=%fused_computation.15 | convolution fusion | flops 1075904512 | bytes 4358144 | tf_op jit(solution)/shard_map/dot_general | solution.py:41
  98.2 0.0 all-gather.5.cloned.1.call-update
  98.2 0.0 reduce-scatter.2.cloned.1.call-start
  98.3 0.7 constant_dynamic-update-slice_fusion.9
  99.0 0.0 collective-permute-done.6
  99.0 0.7 constant_dynamic-update-slice_fusion.8
  99.6 0.7 constant_dynamic-update-slice_fusion.7
  100.3 0.7 constant_dynamic-update-slice_fusion.6
  101.0 0.7 constant_dynamic-update-slice_fusion.5
  101.7 0.7 constant_dynamic-update-slice_fusion.4
  102.3 0.0 copy-done
  102.4 0.7 constant_dynamic-update-slice_fusion.3
  103.0 0.7 constant_dynamic-update-slice_fusion.2
  103.7 0.7 constant_dynamic-update-slice_fusion.1
  104.4 0.7 constant_dynamic-update-slice_fusion
  105.1 6.2 %fusion.27 = (f32[256]{0:T(256)S(1)}, f32[256,2048]{1,0:T(8,128)S(1)}) fusion(bf16[2048,2048]{1,0:T(8,128)(2,1)} %param.9, bf16[256,4096]{1,0:T(8,128)(2,1)} %constant_dynamic-update-slice_fusion, s32[]{:T(128)S(6)} %select_n.31), kind=kOutput, calls=%fused_computation.64 | convolution fusion | flops 2148007680 | bytes 11535364 | tf_op jit(solution)/shard_map/dot_general | solution.py:47
  111.3 0.0 copy-start.1
  111.3 0.0 copy-start.2
  111.3 11.5 %all-gather.5.cloned.1.call-done = bf16[256,2048]{1,0:T(8,128)(2,1)} async-done(((bf16[256,256]{1,0:T(8,128)(2,1)}), bf16[256,2048]{1,0:T(8,128)(2,1)}) %all-gather.5.cloned.1.call-update) | async-done | bytes 1048592 | tf_op jit(solution)/shard_map/all_gather | solution.py:43
  122.8 7.4 %fusion.26 = (f32[256]{0:T(256)S(1)}, f32[256,2048]{1,0:T(8,128)}) fusion(bf16[256,2048]{1,0:T(8,128)(2,1)} %all-gather.5.cloned.1.call-done, bf16[2048,2048]{1,0:T(8,128)(2,1)} %param.9), kind=kOutput, calls=%fused_computation.63 | convolution fusion | flops 2148007680 | bytes 11535360 | tf_op jit(solution)/shard_map/dot_general | solution.py:46
  130.2 14.3 %all-reduce.1 = (f32[256]{0:T(256)S(1)}, f32[256]{0:T(256)S(1)}) all-reduce(f32[256]{0:T(256)S(1)} %get-tuple-element.18, f32[256]{0:T(256)S(1)} %get-tuple-element.20), channel_id=1, replica_groups=mesh['tok'=32,'voc'=8] {'voc'}, use_global_device_ids=true, to_apply=%region_1.2 | all-reduce | flops 512 | bytes 4096 | tf_op jit(solution)/shard_map/pmax | solution.py:51
  144.5 0.0 copy-done.1
  144.5 0.0 copy-done.2
  144.5 3.0 %multiply_reduce_fusion = (f32[256]{0:T(256)S(1)}, f32[256]{0:T(256)S(1)}, f32[256]{0:T(256)S(1)}, f32[256]{0:T(256)S(1)}, f32[256]{0:T(256)S(1)}) fusion(f32[256,2048]{1,0:T(8,128)} %get-tuple-element.19, f32[256,2048]{1,0:T(8,128)S(1)} %get-tuple-element.21, f32[256]{0:T(256)S(1)} %get-tuple-element.12, s32[2048]{0:T(1024)S(1)} %copy-done.1, ...), kind=kLoop, calls=%fused_computation.11 | loop fusion | flops 6290176 | bytes 4210688 | tf_op jit(solution)/shard_map/reduce_sum | solution.py:60
  147.5 12.6 %all-reduce = (f32[256]{0:T(256)S(1)}, f32[256]{0:T(256)S(1)}, f32[256]{0:T(256)S(1)}, f32[256]{0:T(256)S(1)}, f32[256]{0:T(256)S(1)}) all-reduce(f32[256]{0:T(256)S(1)} %get-tuple-element.6, f32[256]{0:T(256)S(1)} %get-tuple-element.4, f32[256]{0:T(256)S(1)} %get-tuple-element.5, ...), channel_id=1, replica_groups=mesh['tok'=32,'voc'=8] {'voc'}, use_global_device_ids=true, to_apply=%region_11.12 | all-reduce | flops 1280 | bytes 10240 | tf_op jit(solution)/shard_map/psum | solution.py:56
  160.2 1.1 broadcast_add_fusion
  161.3 8.3 %convolution_bitcast_fusion = f32[2048,256]{0,1:T(8,128)} fusion(bf16[2048,2048]{1,0:T(8,128)(2,1)} %param.9, f32[256,2048]{1,0:T(8,128)} %get-tuple-element.19, f32[256,2048]{1,0:T(8,128)S(1)} %get-tuple-element.21, f32[256]{0:T(256)S(1)} %get-tuple-element.10, f32[256]{0:T(256)S(1)} %get-tuple-element.9, f32[256]{0:T(256)S(1)} %get-tuple-element.14, ...), kind=kOutput, calls=%fused_computation.6 | convolution fusion | flops 2153250816 | bytes 14695424 | tf_op jit(solution)/shard_map/dot_general | solution.py:78
  169.6 0.0 reduce-scatter.2.cloned.1.call-update
  169.6 35.1 %reduce-scatter.2.cloned.1.call-done = f32[256,256]{0,1:T(8,128)} async-done(((f32[2048,256]{0,1:T(8,128)}), f32[256,256]{0,1:T(8,128)}) %reduce-scatter.2.cloned.1.call-update) | async-done | bytes 262160 | tf_op jit(solution)/shard_map/reduce_scatter | solution.py:77
  204.8 1.6 fusion.19
  (2 shorter events, 0.0 us)
Async XLA Ops:
  7.2 86.9 %all-gather.3.cloned.1.call-start = ((), (), s32[]{:S(2)}) async-start(), calls=%async_computation.1 | async-start | bytes 4325376 | tf_op jit(solution)/shard_map/all_gather | solution.py:37
  7.9 114.9 %all-gather.5.cloned.1.call-start = ((), (), s32[]{:S(2)}) async-start(), calls=%async_computation.2 | async-start | bytes 1179648 | tf_op jit(solution)/shard_map/all_gather | solution.py:43
  7.9 5.8 %collective-permute-start = (bf16[256,256]{1,0:T(8,128)(2,1)}, bf16[256,256]{1,0:T(8,128)(2,1)S(1)}, u32[]{:S(2)}, u32[]{:S(2)}) collective-permute-start(bf16[256,256]{1,0:T(8,128)(2,1)} %param.8), channel_id=1, source_target_pairs={{0,1},{1,2},{2,3},{3,4},{4,5},{5,6},{6,7},{7,0},{8,9},{9,10},{10,1... | collective-permute-start | bytes 393224 | tf_op jit(solution)/shard_map/ppermute | solution.py:15
  13.8 5.6 %collective-permute-start.1 = (bf16[256,256]{1,0:T(8,128)(2,1)S(1)}, bf16[256,256]{1,0:T(8,128)(2,1)S(1)}, u32[]{:S(2)}, u32[]{:S(2)}) collective-permute-start(bf16[256,256]{1,0:T(8,128)(2,1)S(1)} %collective-permute-done), channel_id=1, source_target_pairs={{0,1},{1,2},{2,3},{3,4},{4,5},{5,6},{6,7},{7,0},{8,9},{9,10},{10,1... | collective-permute-start | bytes 393224 | tf_op jit(solution)/shard_map/ppermute | solution.py:15
  13.8 52.0 %collective-permute-start.4 = (bf16[256,256]{1,0:T(8,128)(2,1)}, bf16[256,256]{1,0:T(8,128)(2,1)S(1)}, u32[]{:S(2)}, u32[]{:S(2)}) collective-permute-start(bf16[256,256]{1,0:T(8,128)(2,1)} %param.8), channel_id=1, source_target_pairs={{0,7},{1,0},{2,1},{3,2},{4,3},{5,4},{6,5},{7,6},{8,15},{9,8},{10,9... | collective-permute-start | bytes 393224 | tf_op jit(solution)/shard_map/ppermute | solution.py:17
  19.4 46.5 %collective-permute-start.2 = (bf16[256,256]{1,0:T(8,128)(2,1)S(1)}, bf16[256,256]{1,0:T(8,128)(2,1)S(1)}, u32[]{:S(2)}, u32[]{:S(2)}) collective-permute-start(bf16[256,256]{1,0:T(8,128)(2,1)S(1)} %collective-permute-done.1), channel_id=1, source_target_pairs={{0,1},{1,2},{2,3},{3,4},{4,5},{5,6},{6,7},{7,0},{8,9},{9,10},{10,1... | collective-permute-start | bytes 393224 | tf_op jit(solution)/shard_map/ppermute | solution.py:15
  65.8 2.5 %collective-permute-start.5 = (bf16[256,256]{1,0:T(8,128)(2,1)S(1)}, bf16[256,256]{1,0:T(8,128)(2,1)S(1)}, u32[]{:S(2)}, u32[]{:S(2)}) collective-permute-start(bf16[256,256]{1,0:T(8,128)(2,1)S(1)} %collective-permute-done.4), channel_id=1, source_target_pairs={{0,7},{1,0},{2,1},{3,2},{4,3},{5,4},{6,5},{7,6},{8,15},{9,8},{10,9... | collective-permute-start | bytes 393224 | tf_op jit(solution)/shard_map/ppermute | solution.py:17
  65.8 6.0 %collective-permute-start.3 = (bf16[256,256]{1,0:T(8,128)(2,1)S(1)}, bf16[256,256]{1,0:T(8,128)(2,1)S(1)}, u32[]{:S(2)}, u32[]{:S(2)}) collective-permute-start(bf16[256,256]{1,0:T(8,128)(2,1)S(1)} %collective-permute-done.2), channel_id=1, source_target_pairs={{0,1},{1,2},{2,3},{3,4},{4,5},{5,6},{6,7},{7,0},{8,9},{9,10},{10,1... | collective-permute-start | bytes 393224 | tf_op jit(solution)/shard_map/ppermute | solution.py:15
  68.3 30.6 %collective-permute-start.6 = (bf16[256,256]{1,0:T(8,128)(2,1)S(1)}, bf16[256,256]{1,0:T(8,128)(2,1)S(1)}, u32[]{:S(2)}, u32[]{:S(2)}) collective-permute-start(bf16[256,256]{1,0:T(8,128)(2,1)S(1)} %collective-permute-done.5), channel_id=1, source_target_pairs={{0,7},{1,0},{2,1},{3,2},{4,3},{5,4},{6,5},{7,6},{8,15},{9,8},{10,9... | collective-permute-start | bytes 393224 | tf_op jit(solution)/shard_map/ppermute | solution.py:17
  94.1 8.3 %copy-start = (bf16[256,256]{1,0:T(8,128)(2,1)S(1)}, bf16[256,256]{1,0:T(8,128)(2,1)}, u32[]{:S(2)}) copy-start(bf16[256,256]{1,0:T(8,128)(2,1)} %param.8) | copy-start | bytes 393220
  98.2 106.5 %reduce-scatter.2.cloned.1.call-start = ((), (), s32[]{:S(2)}) async-start(), calls=%async_computation.3 | async-start | bytes 2359296 | tf_op jit(solution)/shard_map/reduce_scatter | solution.py:77
  111.3 33.2 %copy-start.1 = (s32[2048]{0:T(1024)S(1)}, s32[2048]{0:T(1024)}, u32[]{:S(2)}) copy-start(s32[2048]{0:T(1024)} %param.10) | copy-start | bytes 24580
  111.3 33.2 %copy-start.2 = (s32[256]{0:T(256)S(1)}, s32[256]{0:T(256)}, u32[]{:S(2)}) copy-start(s32[256]{0:T(256)} %param.11) | copy-start | bytes 3076
Sparse Core Ops, SparseCore 0:
  10.6 83.4 all-gather.2
  98.3 24.4 all-gather.4
  169.8 34.9 reduce-scatter.1
